TPU v7x, 32 devices: a whole 2x2x4 slice. The times are simulated.
32 devices in a mesh: groups: 2 (over y), ctx: 4 (over z), exp: 4 (over x, core), rep: 1.
Axes of the slice: x: 2, y: 2, z: 4, core: 2. Of those that a mesh axis runs over, the one named last changes fastest.
Arguments:
- queries: bfloat16 [2, 256, 4096], P('groups', 'ctx', ('exp', 'rep')), parts along dimension 0, may hold values from -16.25 to 16.25
- pages: bfloat16 [2, 2304, 2, 512], P('groups', 'ctx', None, 'exp'), parts along dimension 0, may hold values from -5.2 to 5.2
- cached_lengths: int32 [2, 4], P('groups'), parts along dimension 0, may hold values from 128 to 512
- residual_in: bfloat16 [2, 256, 2048], P('groups', ('ctx', 'exp')), parts along dimension 0, may hold values from -2.390625 to 2.390625
- out_weight: bfloat16 [4096, 2048], P(('exp', 'rep')), may hold values from -0.09375 to 0.09375
- norm_gain: float32 [2048], replicated, may hold values from 0.1 to 1.9
- expert_ids: int32 [2, 256, 8], P('groups', ('ctx', 'exp')), parts along dimension 0, may hold values from 0 to 15, all different within a row; in each aligned block of 16 rows (0 to 15, 16 to 31, ..., all dimensions but the last counted through in order) at most 8 rows name the same one
- route_scores: float32 [2, 256, 8], P('groups', ('ctx', 'exp')), parts along dimension 0, may hold values from 0.05 to 1
- expert_input: bfloat16 [16, 2048, 2, 384], P(('ctx', 'exp'), None, None, 'rep'), may hold values from -0.125 to 0.125
- expert_output: bfloat16 [16, 384, 2048], P(('ctx', 'exp'), 'rep'), may hold values from -0.3125 to 0.3125
Outputs:
- context: bfloat16 [2, 256, 4096], P('groups', 'ctx', ('exp', 'rep')), parts along dimension 0
- layer_out: bfloat16 [2, 256, 2048], P('groups', ('ctx', 'exp', 'rep')), parts along dimension 0
There are 2 independent parts, one for each index of `groups`. A program takes and returns all parts, laid end to end along the dimension named above; an argument that names none is the same for every part. Nothing has to cross between parts.
Inputs may be any that keep to these rules, and one draw needn't show every extreme that they name: `expert_ids`: in every aligned block of 16 positions of one request, no expert is named by more than 8 of the block's rows, and in some blocks one expert by exactly 8; the 8 experts of a row differ.
All inputs are finite; a program needn't handle non-finite values.
Results may differ from a plain program's by a relative error of at most 0.015.
Values may be sent and summed in bfloat16 or wider, within the bound.
A program may use at most 128 MiB of HBM per device.

v0:
```python
import jax
import jax.numpy as jnp
from jax import lax
from jax.sharding import PartitionSpec as P

HEAD = 128


floor_value = -1e30
norm_epsilon = 1e-06


def normalize(hidden, norm_gain):
    widened = hidden.astype(jnp.float32)
    mean_square = jnp.mean(widened * widened, axis=-1, keepdims=True)
    return (widened * lax.rsqrt(mean_square + norm_epsilon) * norm_gain).astype(jnp.bfloat16)


def attend_piece(query_rows, page_rows, allowed):
    scaling = query_rows.shape[-1] ** (-0.5)
    scores = (
        jnp.einsum(
            "rqhe,rke->rqhk", query_rows, page_rows[:, :, 0], preferred_element_type=jnp.float32
        )
        * scaling
    )
    permitted = allowed[:, :, None, :]
    masked = jnp.where(permitted, scores, floor_value)
    peaks = jnp.max(masked, axis=-1)
    weights = jnp.where(permitted, jnp.exp(masked - peaks[..., None]), 0.0)
    totals = jnp.sum(weights, axis=-1)
    summed = jnp.einsum(
        "rqhk,rke->rqhe",
        weights.astype(jnp.bfloat16),
        page_rows[:, :, 1],
        preferred_element_type=jnp.float32,
    )
    return (peaks, totals, summed)


def merge_partials(earlier, later):
    peaks = jnp.maximum(earlier[0], later[0])
    later_scale = jnp.exp(later[0] - peaks)
    totals = later[1] * later_scale
    summed = later[2] * later_scale[..., None]
    return (peaks, totals, summed)


def rows_mask(row_index, lengths, query_positions, slab_size, fresh_block):
    page_size = slab_size + fresh_block
    page_number = row_index // page_size
    offset = row_index - page_number * page_size
    page_count = lengths.shape[1]
    picker = page_number[None, :] == jnp.arange(page_count, dtype=jnp.int32)[:, None]
    live_length = jnp.sum(jnp.where(picker[None], lengths[:, :, None], 0), axis=1)
    in_cache = (offset < slab_size)[None, :] & (offset[None, :] < live_length)
    fresh_position = page_number * fresh_block + offset - slab_size
    in_fresh = (offset >= slab_size)[None, :] & (
        fresh_position[None, :] <= query_positions[:, None]
    )
    return in_cache[:, None, :] | in_fresh[None, :, :]


def per_device(
    queries,
    pages,
    cached_lengths,
    residual_in,
    out_weight,
    norm_gain,
    expert_ids,
    route_scores,
    expert_input,
    expert_output,
):
    requests, fresh_block, query_width = queries.shape
    local_heads = query_width // HEAD
    core_place = lax.axis_index("rep")
    page_place = lax.axis_index("ctx")
    rep_count = lax.axis_size("rep")
    page_size = pages.shape[1]
    slab_size = page_size - fresh_block
    own_positions = page_place * fresh_block + jnp.arange(fresh_block, dtype=jnp.int32)
    query_rows = queries.reshape(requests, fresh_block, local_heads, HEAD)
    start_state = (
        jnp.full((requests, fresh_block, local_heads), floor_value, jnp.float32),
        jnp.zeros((requests, fresh_block, local_heads), jnp.float32),
        jnp.zeros((requests, fresh_block, local_heads, HEAD), jnp.float32),
    )
    page_piece = lax.all_gather(pages, "ctx", axis=1, tiled=True)
    row_index = jnp.arange(page_piece.shape[1], dtype=jnp.int32)
    allowed = rows_mask(row_index, cached_lengths, own_positions, slab_size, fresh_block)
    peaks, totals, summed = merge_partials(
        start_state, attend_piece(query_rows, page_piece, allowed)
    )
    context = (
        (summed / totals[..., None])
        .astype(jnp.bfloat16)
        .reshape(requests, fresh_block, query_width)
    )
    projected = jnp.dot(
        context.reshape(requests * fresh_block, query_width),
        out_weight,
        preferred_element_type=jnp.float32,
    ).reshape(requests, fresh_block, -1)
    token_block = residual_in.shape[1]
    share_size = token_block // rep_count
    own_share = lax.psum_scatter(
        projected.astype(jnp.bfloat16), ("exp", "rep"), scatter_dimension=1, tiled=True
    ).astype(jnp.float32)
    own_residual = lax.dynamic_slice_in_dim(residual_in, core_place * share_size, share_size, 1)
    own_hidden = (own_residual.astype(jnp.float32) + own_share).astype(jnp.bfloat16)
    normed = lax.all_gather(normalize(own_hidden, norm_gain), "rep", axis=1, tiled=True)
    top_count = expert_ids.shape[2]
    expert_count = lax.axis_size("ctx") * lax.axis_size("exp")
    most_rows = max(2, (token_block * top_count + expert_count - 1) // expert_count)
    capacity = requests * most_rows
    model_width = normed.shape[2]
    token_count = requests * token_block
    flat_ids = expert_ids.reshape(-1)
    row_count = flat_ids.shape[0]
    chosen = (flat_ids[:, None] == jnp.arange(expert_count, dtype=jnp.int32)[None, :]).astype(
        jnp.int32
    )
    earlier_rows = jnp.cumsum(chosen, axis=0) - chosen
    slot_rank = jnp.sum(earlier_rows * chosen, axis=1)
    slot_index = flat_ids * capacity + slot_rank
    slot_onehot = (
        slot_index[:, None] == jnp.arange(expert_count * capacity, dtype=jnp.int32)[None, :]
    ).astype(jnp.bfloat16)
    token_onehot = (
        (jnp.arange(row_count, dtype=jnp.int32) // top_count)[:, None]
        == jnp.arange(token_count, dtype=jnp.int32)[None, :]
    ).astype(jnp.bfloat16)
    placement = jnp.dot(slot_onehot.T, token_onehot, preferred_element_type=jnp.float32).astype(
        jnp.bfloat16
    )
    outgoing = jnp.dot(
        placement, normed.reshape(token_count, model_width), preferred_element_type=jnp.float32
    )
    outgoing = outgoing.astype(jnp.bfloat16).reshape(expert_count, capacity, model_width)
    scores_sum = jnp.sum(route_scores, axis=2, keepdims=True)
    combine = (route_scores / scores_sum).astype(jnp.bfloat16).reshape(-1)
    gathering = jnp.dot(
        (token_onehot * combine[:, None]).T, slot_onehot, preferred_element_type=jnp.float32
    ).astype(jnp.bfloat16)
    gate_up = expert_input[0]
    down_weight = expert_output[0]
    arrived_rows = lax.all_to_all(outgoing, ("ctx", "exp"), split_axis=0, concat_axis=0, tiled=True)
    inner_rows = jnp.einsum(
        "nd,dgh->ngh",
        arrived_rows.reshape(-1, model_width),
        gate_up,
        preferred_element_type=jnp.float32,
    )
    activated = (jax.nn.silu(inner_rows[:, 0]) * inner_rows[:, 1]).astype(jnp.bfloat16)
    result = jnp.dot(activated, down_weight, preferred_element_type=jnp.float32).astype(
        jnp.bfloat16
    )
    returned = lax.all_to_all(
        result.reshape(arrived_rows.shape), ("ctx", "exp"), split_axis=0, concat_axis=0, tiled=True
    )
    mixture = jnp.dot(
        gathering,
        returned.reshape(expert_count * capacity, model_width),
        preferred_element_type=jnp.float32,
    )
    own_mixture = lax.psum_scatter(
        mixture.reshape(requests, token_block, model_width).astype(jnp.bfloat16),
        "rep",
        scatter_dimension=1,
        tiled=True,
    ).astype(jnp.float32)
    layer_out = (own_hidden.astype(jnp.float32) + own_mixture).astype(jnp.bfloat16)
    return (context, layer_out)


def solution(mesh):
    in_specs = (
        P("groups", "ctx", ("exp", "rep")),
        P("groups", "ctx", None, "exp"),
        P("groups", None),
        P("groups", ("ctx", "exp"), None),
        P(("exp", "rep"), None),
        P(),
        P("groups", ("ctx", "exp"), None),
        P("groups", ("ctx", "exp"), None),
        P(("ctx", "exp"), None, None, "rep"),
        P(("ctx", "exp"), "rep", None),
    )
    out_specs = (P("groups", "ctx", ("exp", "rep")), P("groups", ("ctx", "exp", "rep"), None))
    return jax.shard_map(
        per_device, mesh=mesh, in_specs=in_specs, out_specs=out_specs, check_vma=False
    )
```

profile of v0, /device:TPU:0, one launch (start us, length us, event | category | flops | bytes accessed | tf_op | source)
XLA Modules:
  0.0 121.3 jit_solution(10408529155012849360)
XLA Ops:
  7.2 1.9 %copy.20 = bf16[1,576,2,128]{3,1,2,0:T(8,128)(2,1)} copy(bf16[1,576,2,128]{3,2,1,0:T(2,128)(2,1)} %param.11) | data formatting | bytes 589824 | tf_op args[1]
  9.2 0.9 copy.24
  10.1 0.8 copy.22
  11.0 0.8 select_reduce_fusion.1
  11.8 0.2 and_or_fusion
  12.0 30.6 %all-gather.2.cloned.1.call-done = bf16[1,2304,2,128]{3,1,2,0:T(8,128)(2,1)} async-done(((bf16[1,576,2,128]{3,1,2,0:T(8,128)(2,1)}), bf16[1,2304,2,128]{3,1,2,0:T(8,128)(2,1)}) %all-gather.2.cloned.1.call-update) | async-done | bytes 1179664 | tf_op jit(solution)/shard_map/all_gather | solution.py:90
  42.6 2.5 %fusion.70 = (f32[64,8]{1,0:T(8,128)S(1)}, f32[64,8,2304]{2,1,0:T(8,128)S(1)}) fusion(bf16[64,8,128]{2,1,0:T(8,128)(2,1)S(1)} %bitcast.57, bf16[1,2304,2,128]{3,1,2,0:T(8,128)(2,1)} %all-gather.2.cloned.1.call-done, pred[64,2304]{1,0:T(8,128)(4,1)S(1)} %and_or_fusion), kind=kOutput, calls=%fused_computation.88 | convolution fusion | flops 305528320 | bytes 5588992 | tf_op jit(solution)/shard_map/rqhe,rke->rqhk/dot_general | solution.py:22
  45.1 1.3 %fusion.1 = f32[64,8]{1,0:T(8,128)S(1)} fusion(f32[64,8,2304]{2,1,0:T(8,128)S(1)} %get-tuple-element.5, f32[64,8]{1,0:T(8,128)S(1)} %get-tuple-element.4, pred[64,2304]{1,0:T(8,128)(4,1)S(1)} %and_or_fusion), kind=kLoop, calls=%fused_computation.3 | loop fusion | flops 3538432 | bytes 4870144 | tf_op jit(solution)/shard_map/reduce_sum | solution.py:31
  46.4 1.1 fusion.24
  47.5 1.0 copy-done.1
  48.5 1.5 %fusion.12 = bf16[1,64,2048]{2,1,0:T(8,128)(2,1)} fusion(bf16[1024,2048]{1,0:T(8,128)(2,1)S(1)} %copy-done.1, bf16[8,8,8,128]{3,2,1,0:T(8,128)(2,1)S(1)} %bitcast.56), kind=kOutput, calls=%fused_computation.16 | convolution fusion | flops 268566528 | bytes 4587520 | tf_op jit(solution)/shard_map/dot_general | solution.py:101
  50.2 0.2 reduce_window_sum.11
  50.4 0.2 select_reduce_fusion
  50.6 19.0 %reduce-scatter.2.cloned.1.call-done = bf16[1,16,2048]{2,1,0:T(8,128)(2,1)} async-done(((bf16[1,64,2048]{2,1,0:T(8,128)(2,1)}), bf16[1,16,2048]{2,1,0:T(8,128)(2,1)}) %reduce-scatter.2.cloned.1.call-update) | async-done | bytes 65552 | tf_op jit(solution)/shard_map/reduce_scatter | solution.py:108
  69.6 1.0 fusion.30
  70.6 2.2 %fusion.10 = bf16[16,8,2048]{2,1,0:T(8,128)(2,1)} fusion(f32[2048]{0:T(1024)S(1)} %copy-done.7, f32[16]{0:T(128)S(1)} %add_rsqrt_fusion, s32[128]{0:T(128)S(1)} %get-tuple-element.9, s32[128]{0:T(128)S(1)} %get-tuple-element.8, bf16[1,16,2048]{2,1,0:T(8,128)(2,1)} %reduce-scatter.2.cloned.1.call-done, bf16[1,16,2048]{2,1,0:T(8,128)(2,1)S(1)} %copy-done.3), kind=kOutput, calls=%fused_computation.13 | convolution fusion | flops 9457664 | bytes 664640 | tf_op jit(solution)/shard_map/dot_general | solution.py:138
  72.8 19.1 %all_to_all.10 = bf16[16,8,2048]{2,1,0:T(8,128)(2,1)S(1)} all-to-all(bf16[16,8,2048]{2,1,0:T(8,128)(2,1)} %fusion.10), channel_id=1, replica_groups=mesh['groups'=2,'ctx'=4,'exp'=4,'rep'=1] {'ctx','exp'}, dimensions={0} | all-to-all | bytes 1048576 | tf_op jit(solution)/shard_map/all_to_all | solution.py:149
  91.9 0.6 fusion.3
  92.5 1.3 %fusion.11 = bf16[16,8,2048]{2,1,0:T(8,128)(2,1)} fusion(bf16[1,384,2048]{2,1,0:T(8,128)(2,1)S(1)} %copy-done.2, f32[128,2,384]{2,0,1:T(8,128)S(1)} %fusion.3), kind=kOutput, calls=%fused_computation.14 | convolution fusion | flops 201883648 | bytes 2490368 | tf_op jit(solution)/shard_map/dot_general | solution.py:157
  93.8 4.2 %all-to-all-start.1 = ((bf16[16,8,2048]{2,1,0:T(8,128)(2,1)}), bf16[16,8,2048]{2,1,0:T(8,128)(2,1)}, u32[]{:S(2)}, u32[]{:S(2)}) async-start(bf16[16,8,2048]{2,1,0:T(8,128)(2,1)} %fusion.11), calls=%async_computation.2 | async-start | bytes 1048576 | tf_op jit(solution)/shard_map/all_to_all | solution.py:160
  98.2 0.1 mul.119
  98.3 0.7 reshape.326
  99.0 13.4 %all-to-all-done.1 = bf16[16,8,2048]{2,1,0:T(8,128)(2,1)} async-done(((bf16[16,8,2048]{2,1,0:T(8,128)(2,1)}), bf16[16,8,2048]{2,1,0:T(8,128)(2,1)}, u32[]{:S(2)}, u32[]{:S(2)}) %all-to-all-start.1) | async-done | bytes 524320 | tf_op jit(solution)/shard_map/all_to_all | solution.py:160
  112.4 2.1 %fusion.16 = bf16[1,16,2048]{2,1,0:T(8,128)(2,1)} fusion(bf16[16,8,2048]{2,1,0:T(8,128)(2,1)} %all-to-all-done.1, s32[128]{0:T(128)S(1)} %get-tuple-element.9, s32[128]{0:T(128)S(1)} %get-tuple-element.8, bf16[128]{0:T(256)(128)(2,1)S(1)} %mul.119, bf16[1,16,2048]{2,1,0:T(8,128)(2,1)S(1)} %copy-done.4, bf16[1,16,2048]{2,1,0:T(8,128)(2,1)S(1)} %copy-done.3), kind=kOutput, calls=%fused_computation.21 | convolution fusion | flops 9230336 | bytes 722176 | tf_op jit(solution)/shard_map/dot_general | solution.py:163
  (31 shorter events, 0.5 us)
Async XLA Ops:
  7.2 84.7 %copy-start = (bf16[1,2048,2,384]{3,2,1,0:T(2,128)(2,1)S(1)}, bf16[1,2048,2,384]{3,2,1,0:T(2,128)(2,1)}, u32[]{:S(2)}) copy-start(bf16[1,2048,2,384]{3,2,1,0:T(2,128)(2,1)} %param.18) | copy-start | bytes 9437188
  7.2 35.4 %all-gather.2.cloned.1.call-start = ((), (), s32[]{:S(2)}) async-start(), calls=%async_computation.3 | async-start | bytes 1474560 | tf_op jit(solution)/shard_map/all_gather | solution.py:90
  9.1 60.5 %reduce-scatter.2.cloned.1.call-start = ((), (), s32[]{:S(2)}) async-start(), calls=%async_computation.4 | async-start | bytes 327680 | tf_op jit(solution)/shard_map/reduce_scatter | solution.py:108
  42.6 3.8 %copy-start.5 = (bf16[1,2304,2,128]{3,1,2,0:T(8,128)(2,1)S(1)}, bf16[1,2304,2,128]{3,1,2,0:T(8,128)(2,1)}, u32[]{:S(2)}) copy-start(bf16[1,2304,2,128]{3,1,2,0:T(8,128)(2,1)} %all-gather.2.cloned.1.call-done) | copy-start | bytes 3538948
  46.4 2.2 %copy-start.1 = (bf16[1024,2048]{1,0:T(8,128)(2,1)S(1)}, bf16[1024,2048]{1,0:T(8,128)(2,1)}, u32[]{:S(2)}) copy-start(bf16[1024,2048]{1,0:T(8,128)(2,1)} %param.14) | copy-start | bytes 12582916
  47.5 22.1 %copy-start.3 = (bf16[1,16,2048]{2,1,0:T(8,128)(2,1)S(1)}, bf16[1,16,2048]{2,1,0:T(8,128)(2,1)}, u32[]{:S(2)}) copy-start(bf16[1,16,2048]{2,1,0:T(8,128)(2,1)} %param.13) | copy-start | bytes 196612
  47.5 23.1 %copy-start.7 = (f32[2048]{0:T(1024)S(1)}, f32[2048]{0:T(1024)}, u32[]{:S(2)}) copy-start(f32[2048]{0:T(1024)} %param.15) | copy-start | bytes 24580
  72.8 19.8 %copy-start.2 = (bf16[1,384,2048]{2,1,0:T(8,128)(2,1)S(1)}, bf16[1,384,2048]{2,1,0:T(8,128)(2,1)}, u32[]{:S(2)}) copy-start(bf16[1,384,2048]{2,1,0:T(8,128)(2,1)} %param.19) | copy-start | bytes 4718596
  91.9 6.2 %copy-start.6 = (f32[1,16,8]{1,2,0:T(8,128)S(1)}, f32[1,16,8]{1,2,0:T(8,128)}, u32[]{:S(2)}) copy-start(f32[1,16,8]{1,2,0:T(8,128)} %param.17) | copy-start | bytes 1540
  91.9 20.5 %copy-start.4 = (bf16[1,16,2048]{2,1,0:T(8,128)(2,1)S(1)}, bf16[1,16,2048]{2,1,0:T(8,128)(2,1)}, u32[]{:S(2)}) copy-start(bf16[1,16,2048]{2,1,0:T(8,128)(2,1)} %reduce-scatter.2.cloned.1.call-done) | copy-start | bytes 196612
  93.8 18.6 %all-to-all-start.1 = ((bf16[16,8,2048]{2,1,0:T(8,128)(2,1)}), bf16[16,8,2048]{2,1,0:T(8,128)(2,1)}, u32[]{:S(2)}, u32[]{:S(2)}) async-start(bf16[16,8,2048]{2,1,0:T(8,128)(2,1)} %fusion.11), calls=%async_computation.2 | async-start | bytes 1048576 | tf_op jit(solution)/shard_map/all_to_all | solution.py:160
Sparse Core Ops, SparseCore 0:
  9.6 32.9 all-gather.1
  50.2 19.2 reduce-scatter.1
where the time goes:
time: 122 us; the launch traced here: 121 us
  waiting for transfers between devices  63 us (52%)
  blocking collectives  19.1 us (16%)
  between operations  14.2 us (12%)
  matrix products  11.3 us (9%)
  local copies, waits for them, and re-layouts  5.62 us (5%)
  starting transfers between devices  4.32 us (4%)
  other arithmetic  3.74 us (3%)
    all_gather x1, waiting for transfers between devices, per_device(): page_piece = lax.all_gather(pages, 'ctx', axis=1, tiled=True)  30.6 us
    all_to_all x1, blocking collectives, per_device(): lax.all_to_all(outgoing, ('ctx', 'exp'), split_axis=0, concat_axis=0, til...  19.1 us
    reduce_scatter x1, waiting for transfers between devices, per_device(): lax.psum_scatter(projected.astype(jnp.bfloat16), ('exp', 'rep'), scatter_...  19 us
    all_to_all x1, waiting for transfers between devices, per_device(): lax.all_to_all(result.reshape(arrived_rows.shape), ('ctx', 'exp'), split_...  13.4 us
    unnamed x19, local copies, waits for them, and re-layouts  4.63 us
    all_to_all x1, starting transfers between devices, per_device(): lax.all_to_all(result.reshape(arrived_rows.shape), ('ctx', 'exp'), split_...  4.24 us
    dot_general x1, matrix products, attend_piece(): jnp.einsum('rqhe,rke->rqhk', query_rows, page_rows[:, :, 0], preferred_el...  2.46 us
  transfers between devices with their start and end apart: 3, of which 3 were waited for; matrix products, arithmetic and copies ran while one was open for 3% of the time, Pallas kernels for 0%

commit v1 on v0

--- a/solution.py
+++ b/solution.py
@@ -1,6 +1,10 @@
+import functools
+
 import jax
 import jax.numpy as jnp
 from jax import lax
+from jax.experimental import pallas as pl
+from jax.experimental.pallas import tpu as pltpu
 from jax.sharding import PartitionSpec as P
 
 HEAD = 128
@@ -175,6 +179,389 @@
     return (context, layer_out)
 
 
+BF = jnp.bfloat16
+F32 = jnp.float32
+MESH = pl.DeviceIdType.MESH
+VMEM_LIMIT = 60 * 1024 * 1024
+
+
+def fused_kernel(
+    ctx_count, exp_count, capacity,
+    lengths, query, page, residual, gain, ids, scores, w_out, w_in, w_down,
+    context_out, layer_out,
+    kv, q_rows, bias, peak, total, accum, wo, wi, wg, wu, wd,
+    ids_all, scores_all, combine_all, place, gather,
+    rs_full, rs_send, rs_recv, hidden, nz, x_send, x_recv, x_rows, y_send, y_recv, y_rows, mix_send, mix_recv,
+    kv_left, kv_right, kv_recv, w_sem,
+    ids_s, ids_r, sc_s, sc_r, rs_s, rs_r, nz_s, nz_r, dx_s, dx_r, ret_s, ret_r, mix_s, mix_r,
+):
+    ci = lax.axis_index("ctx")
+    ei = lax.axis_index("exp")
+    fresh = query.shape[0]
+    heads = query.shape[1] // HEAD
+    page_size = page.shape[0]
+    slab = page_size - fresh
+    rows = residual.shape[0]
+    width = residual.shape[1]
+    top = ids.shape[1]
+    scaling = HEAD ** (-0.5) * 1.4426950408889634
+
+    def ctx_peer(k):
+        return {"ctx": lax.rem(ci + k, ctx_count)}
+
+    def exp_peer(k):
+        return {"exp": lax.rem(ei + k, exp_count)}
+
+    def remote(src, dst, ss, rs, where):
+        return pltpu.make_async_remote_copy(
+            src_ref=src, dst_ref=dst, send_sem=ss, recv_sem=rs, device_id=where, device_id_type=MESH
+        )
+
+    copies_w = [
+        pltpu.make_async_copy(w_out, wo, w_sem.at[0]),
+        pltpu.make_async_copy(w_in, wi, w_sem.at[1]),
+        pltpu.make_async_copy(w_down, wd, w_sem.at[2]),
+    ]
+
+    barrier = pltpu.get_barrier_semaphore()
+    for k in range(1, ctx_count):
+        pl.semaphore_signal(barrier, inc=1, device_id=ctx_peer(k), device_id_type=MESH)
+    for k in range(1, exp_count):
+        pl.semaphore_signal(barrier, inc=1, device_id=exp_peer(k), device_id_type=MESH)
+    pl.semaphore_wait(barrier, ctx_count + exp_count - 2)
+
+    def right_copy(src, p):
+        return remote(src, kv.at[p], kv_right.at[p], kv_recv.at[p], {"ctx": ci + 1})
+
+    def left_copy(src, p):
+        return remote(src, kv.at[p], kv_left.at[p], kv_recv.at[p], {"ctx": ci - 1})
+
+    @pl.when(ci < ctx_count - 1)
+    def _():
+        right_copy(page, ci).start()
+
+    @pl.when(ci > 0)
+    def _():
+        left_copy(page, ci).start()
+
+    small = []
+    for k in range(1, ctx_count):
+        small.append(remote(ids, ids_all.at[k], ids_s.at[k], ids_r.at[k], ctx_peer(k)))
+        small.append(remote(scores, scores_all.at[k], sc_s.at[k], sc_r.at[k], ctx_peer(k)))
+    for c in small:
+        c.start()
+    for c in copies_w:
+        c.start()
+
+    for h in range(heads):
+        q_rows[h * fresh:(h + 1) * fresh, :] = query[:, h * HEAD:(h + 1) * HEAD]
+    accum[...] = jnp.zeros_like(accum)
+    total[...] = jnp.zeros_like(total)
+    peak[...] = jnp.full_like(peak, floor_value)
+
+    offset = lax.broadcasted_iota(jnp.int32, (fresh, page_size), 1)
+    position = lax.broadcasted_iota(jnp.int32, (fresh, page_size), 0) + ci * fresh
+
+    def attend(source, p):
+        live = lengths[p]
+        cached = (offset < slab) & (offset < live)
+        new = (offset >= slab) & (p * fresh + offset - slab <= position)
+        bias[...] = jnp.where(cached | new, 0.0, floor_value)
+        both = source[...]
+        keys = both[:, 0, :]
+        values = both[:, 1, :]
+        step = 2 if heads % 2 == 0 else 1
+        for h in range(0, heads, step):
+            sl = slice(h * fresh, (h + step) * fresh)
+            s = lax.dot_general(
+                q_rows[sl, :], keys, (((1,), (1,)), ((), ())), preferred_element_type=F32
+            )
+            s = jnp.concatenate([s[i * fresh:(i + 1) * fresh] + bias[...] for i in range(step)], 0)
+            old = peak[sl, :]
+            now = jnp.maximum(old, jnp.max(s, axis=1, keepdims=True))
+            w = jnp.exp2((s - now[:, :1]) * scaling)
+            fade = jnp.exp2((old - now) * scaling)
+            total[sl, :] = total[sl, :] * fade + jnp.sum(w, axis=1, keepdims=True)
+            accum[sl, :] = accum[sl, :] * fade + jnp.dot(
+                w.astype(BF), values, preferred_element_type=F32
+            )
+            peak[sl, :] = now
+
+    attend(page, ci)
+
+    copies_w[1].wait()
+    depth = 256
+
+    def unpack(i, carry):
+        at = pl.ds(pl.multiple_of(i * depth, depth), depth)
+        block = wi[at]
+        wg[at, :] = block[:, 0, :]
+        wu[at, :] = block[:, 1, :]
+        return carry
+
+    lax.fori_loop(0, width // depth, unpack, 0)
+
+    combined = scores[...] / jnp.sum(scores[...], axis=1, keepdims=True)
+    ids_all[0] = ids[...]
+    combine_all[0] = combined.astype(BF).astype(F32)
+    for c in small:
+        c.wait()
+    for k in range(1, ctx_count):
+        given = scores_all[k]
+        combine_all[k] = (given / jnp.sum(given, axis=1, keepdims=True)).astype(BF).astype(F32)
+
+    lanes = exp_count * capacity
+    lane = lax.broadcasted_iota(jnp.int32, (rows, lanes), 1)
+    wanted = ci * exp_count + lax.rem(ei + lane // capacity, exp_count)
+    seat = (lane - lane // capacity * capacity).astype(F32)
+    earlier = (
+        lax.broadcasted_iota(jnp.int32, (rows, rows), 1)
+        < lax.broadcasted_iota(jnp.int32, (rows, rows), 0)
+    ).astype(F32)
+    for k in range(ctx_count):
+        chosen = jnp.zeros((rows, lanes), F32)
+        portion = jnp.zeros((rows, lanes), F32)
+        for j in range(top):
+            hit = ids_all[k, :, j:j + 1] == wanted
+            chosen = jnp.where(hit, 1.0, chosen)
+            portion = jnp.where(hit, combine_all[k, :, j:j + 1], portion)
+        rank = jnp.dot(earlier.astype(BF), chosen.astype(BF), preferred_element_type=F32)
+        seated = (chosen > 0.5) & (rank == seat)
+        place[k] = jnp.where(seated, 1.0, 0.0)
+        gather[k] = jnp.where(seated, portion, 0.0)
+
+    def arrival(i, carry):
+        d = i // 2 + 1
+        p = jnp.where(lax.rem(i, 2) == 0, ci - d, ci + d)
+
+        @pl.when((p >= 0) & (p < ctx_count))
+        def _():
+            right_copy(kv.at[p], p).wait_recv()
+
+            @pl.when((p < ci) & (ci < ctx_count - 1))
+            def _():
+                right_copy(kv.at[p], p).start()
+
+            @pl.when((p > ci) & (ci > 0))
+            def _():
+                left_copy(kv.at[p], p).start()
+
+            attend(kv.at[p], p)
+
+        return carry
+
+    lax.fori_loop(0, 2 * (ctx_count - 1), arrival, 0)
+
+    for h in range(heads):
+        sl = slice(h * fresh, (h + 1) * fresh)
+        context_out[:, h * HEAD:(h + 1) * HEAD] = (accum[sl, :] / total[sl, :]).astype(BF)
+
+    copies_w[0].wait()
+
+    pieces = 4
+    piece = width // pieces
+    own_share = []
+    rs_copies = []
+    for n in range(pieces):
+        cols = slice(n * piece, (n + 1) * piece)
+        part = jnp.dot(context_out[...], wo[:, cols], preferred_element_type=F32)
+        rs_full[n] = part
+        for k in range(1, exp_count):
+            at = pl.ds(pl.multiple_of(lax.rem(ei + k, exp_count) * rows, rows), rows)
+            rs_send[k, n] = rs_full[n, at, :].astype(BF)
+            c = remote(rs_send.at[k, n], rs_recv.at[k, n], rs_s.at[k, n], rs_r.at[k, n], exp_peer(k))
+            c.start()
+            rs_copies.append(c)
+    mine = pl.ds(pl.multiple_of(ei * rows, rows), rows)
+    square = jnp.zeros((rows, 1), F32)
+    for n in range(pieces):
+        cols = slice(n * piece, (n + 1) * piece)
+        share = rs_full[n, mine, :]
+        for k in range(1, exp_count):
+            rs_copies[n * (exp_count - 1) + k - 1].wait_recv()
+            share = share + rs_recv[k, n].astype(F32)
+        h = (residual[:, cols].astype(F32) + share).astype(BF)
+        hidden[:, cols] = h
+        wide = h.astype(F32)
+        square = square + jnp.sum(wide * wide, axis=1, keepdims=True)
+    inverse = lax.rsqrt(square / width + norm_epsilon)
+    nz[0] = (hidden[...].astype(F32) * inverse * gain[...]).astype(BF)
+
+    nz_copies = {}
+    order = [1, ctx_count - 1] + list(range(2, ctx_count - 1)) if ctx_count > 2 else list(range(1, ctx_count))
+    for k in reversed(order):
+        c = remote(nz.at[0], nz.at[k], nz_s.at[k], nz_r.at[k], ctx_peer(k))
+        c.start()
+        nz_copies[k] = c
+
+    dx_copies = []
+    for k in [0] + order:
+        if k:
+            nz_copies[k].wait_recv()
+        routed = lax.dot_general(
+            place[k].astype(BF), nz[k], (((0,), (0,)), ((), ())), preferred_element_type=F32
+        )
+        for j in range(exp_count):
+            block = routed[j * capacity:(j + 1) * capacity].astype(BF)
+            if j == 0:
+                x_recv[0, k] = block
+            else:
+                x_send[j, k] = block
+                c = remote(x_send.at[j, k], x_recv.at[j, k], dx_s.at[j, k], dx_r.at[j, k], exp_peer(j))
+                c.start()
+                dx_copies.append(c)
+    copies_w[2].wait()
+    for c in dx_copies:
+        c.wait_recv()
+    for j in range(exp_count):
+        for k in range(ctx_count):
+            at = slice((j * ctx_count + k) * capacity, (j * ctx_count + k + 1) * capacity)
+            x_rows[at, :] = x_recv[j, k].astype(F32)
+    x = x_rows[...].astype(BF)
+    gate = jnp.dot(x, wg[...], preferred_element_type=F32)
+    up = jnp.dot(x, wu[...], preferred_element_type=F32)
+    act = (gate / (1.0 + jnp.exp(-gate)) * up).astype(BF)
+    span = ctx_count * capacity
+    ret_copies = []
+    result = jnp.dot(act, wd[...], preferred_element_type=F32)
+    for j in range(exp_count):
+        block = result[j * span:(j + 1) * span].astype(BF)
+        if j == 0:
+            y_recv[0] = block
+        else:
+            y_send[j] = block
+            c = remote(y_send.at[j], y_recv.at[j], ret_s.at[j], ret_r.at[j], exp_peer(exp_count - j))
+            c.start()
+            ret_copies.append(c)
+    for c in ret_copies:
+        c.wait_recv()
+    for j in range(exp_count):
+        y_rows[j] = y_recv[j].astype(F32)
+    mix_copies = []
+    own = None
+    for k in list(reversed(order)) + [0]:
+        rows_k = jnp.concatenate(
+            [y_rows[j, k * capacity:(k + 1) * capacity] for j in range(exp_count)], 0
+        ).astype(BF)
+        mixed = jnp.dot(gather[k].astype(BF), rows_k, preferred_element_type=F32)
+        if k == 0:
+            own = mixed
+        else:
+            mix_send[k] = mixed.astype(BF)
+            c = remote(mix_send.at[k], mix_recv.at[k], mix_s.at[k], mix_r.at[k], ctx_peer(ctx_count - k))
+            c.start()
+            mix_copies.append(c)
+    out = hidden[...].astype(F32) + own
+    for c, k in zip(reversed(mix_copies), order):
+        c.wait_recv()
+        out = out + mix_recv[k].astype(F32)
+    layer_out[...] = out.astype(BF)
+
+    for c in rs_copies + list(nz_copies.values()) + dx_copies + ret_copies + mix_copies:
+        c.wait_send()
+
+    @pl.when(ci < ctx_count - 1)
+    def _():
+        right_copy(page, ci).wait_send()
+
+    @pl.when(ci > 0)
+    def _():
+        left_copy(page, ci).wait_send()
+
+    def drain(p, carry):
+        @pl.when((p < ci) & (ci < ctx_count - 1))
+        def _():
+            right_copy(kv.at[p], p).wait_send()
+
+        @pl.when((p > ci) & (ci > 0))
+        def _():
+            left_copy(kv.at[p], p).wait_send()
+
+        return carry
+
+    lax.fori_loop(0, ctx_count, drain, 0)
+
+
+def fused_device(
+    ctx_count, exp_count, queries, pages, cached_lengths, residual_in, out_weight, norm_gain,
+    expert_ids, route_scores, expert_input, expert_output,
+):
+    fresh, query_width = queries.shape[1:]
+    page_size = pages.shape[1]
+    rows, width = residual_in.shape[1:]
+    top = expert_ids.shape[2]
+    hidden_width = expert_input.shape[3]
+    experts = ctx_count * exp_count
+    capacity = max(2, -(-rows * top // experts))
+    stacked = query_width // HEAD * fresh
+    span = ctx_count * capacity
+    vm = pl.BlockSpec(memory_space=pltpu.VMEM)
+    sm = pl.BlockSpec(memory_space=pltpu.SMEM)
+    hbm = pl.BlockSpec(memory_space=pl.ANY)
+    dma = pltpu.SemaphoreType.DMA
+    V = pltpu.VMEM
+    lanes = exp_count * capacity
+    pieces = 4
+    context, layer_out = pl.pallas_call(
+        functools.partial(fused_kernel, ctx_count, exp_count, capacity),
+        out_shape=(
+            jax.ShapeDtypeStruct((fresh, query_width), BF),
+            jax.ShapeDtypeStruct((rows, width), BF),
+        ),
+        in_specs=[sm, vm, vm, vm, vm, vm, vm, hbm, hbm, hbm],
+        out_specs=(vm, vm),
+        scratch_shapes=[
+            V((ctx_count,) + pages.shape[1:], BF),
+            V((stacked, HEAD), BF),
+            V((fresh, page_size), F32),
+            V((stacked, HEAD), F32),
+            V((stacked, HEAD), F32),
+            V((stacked, HEAD), F32),
+            V(out_weight.shape, BF),
+            V(expert_input.shape[1:], BF),
+            V((width, hidden_width), BF),
+            V((width, hidden_width), BF),
+            V(expert_output.shape[1:], BF),
+            V((ctx_count, rows, top), jnp.int32),
+            V((ctx_count, rows, top), F32),
+            V((ctx_count, rows, top), F32),
+            V((ctx_count, rows, lanes), F32),
+            V((ctx_count, rows, lanes), F32),
+            V((pieces, fresh, width // pieces), F32),
+            V((exp_count, pieces, rows, width // pieces), BF),
+            V((exp_count, pieces, rows, width // pieces), BF),
+            V((rows, width), BF),
+            V((ctx_count, rows, width), BF),
+            V((exp_count, ctx_count, capacity, width), BF),
+            V((exp_count, ctx_count, capacity, width), BF),
+            V((exp_count * span, width), F32),
+            V((exp_count, span, width), BF),
+            V((exp_count, span, width), BF),
+            V((exp_count, span, width), F32),
+            V((ctx_count, rows, width), BF),
+            V((ctx_count, rows, width), BF),
+            dma((ctx_count,)), dma((ctx_count,)), dma((ctx_count,)), dma((3,)),
+            dma((ctx_count,)), dma((ctx_count,)), dma((ctx_count,)), dma((ctx_count,)),
+            dma((exp_count, pieces)), dma((exp_count, pieces)),
+            dma((ctx_count,)), dma((ctx_count,)),
+            dma((exp_count, ctx_count)), dma((exp_count, ctx_count)),
+            dma((exp_count,)), dma((exp_count,)),
+            dma((ctx_count,)), dma((ctx_count,)),
+        ],
+        compiler_params=pltpu.CompilerParams(
+            collective_id=0, has_side_effects=True, vmem_limit_bytes=VMEM_LIMIT
+        ),
+    )(
+        cached_lengths[0], queries[0], pages[0], residual_in[0], norm_gain.reshape(1, width),
+        expert_ids[0], route_scores[0], out_weight, expert_input[0], expert_output[0],
+    )
+    return context[None], layer_out[None]
+
+
+def fused_fits(mesh):
+    return mesh.shape["rep"] == 1 and mesh.shape["ctx"] <= 8
+
+
 def solution(mesh):
     in_specs = (
         P("groups", "ctx", ("exp", "rep")),
@@ -189,6 +576,9 @@
         P(("ctx", "exp"), "rep", None),
     )
     out_specs = (P("groups", "ctx", ("exp", "rep")), P("groups", ("ctx", "exp", "rep"), None))
+    body = per_device
+    if fused_fits(mesh):
+        body = functools.partial(fused_device, mesh.shape["ctx"], mesh.shape["exp"])
     return jax.shard_map(
-        per_device, mesh=mesh, in_specs=in_specs, out_specs=out_specs, check_vma=False
-    )
+        body, mesh=mesh, in_specs=in_specs, out_specs=out_specs, check_vma=False
+    )

time: 122 us -> 74 us (0.61)
  Pallas kernels: 0 us -> 67.3 us
  waiting for transfers between devices: 63 us -> 0 us
  blocking collectives: 19.1 us -> 0 us
  between operations: 14.2 us -> 0.64 us
  matrix products: 11.3 us -> 0 us
  starting transfers between devices: 4.32 us -> 0 us
  other arithmetic: 3.74 us -> 0 us
    pallas_call x0 -> x1, Pallas kernels: none -> 67.3 us  [fused_device(): pl.pallas_call(functools.partial(fused_kernel, ctx_count, exp_count, capa...]
    all_gather x1 -> x0, waiting for transfers between devices: 30.6 us -> none  [per_device(): page_piece = lax.all_gather(pages, 'ctx', axis=1, tiled=True)]
    all_to_all x1 -> x0, blocking collectives: 19.1 us -> none  [per_device(): lax.all_to_all(outgoing, ('ctx', 'exp'), split_axis=0, concat_axis=0, til...]
    reduce_scatter x1 -> x0, waiting for transfers between devices: 19 us -> none  [per_device(): lax.psum_scatter(projected.astype(jnp.bfloat16), ('exp', 'rep'), scatter_...]
    all_to_all x1 -> x0, waiting for transfers between devices: 13.4 us -> none  [per_device(): lax.all_to_all(result.reshape(arrived_rows.shape), ('ctx', 'exp'), split_...]
    dot_general x7 -> x0, matrix products: 11.3 us -> none  [the longest x1 2.46 us: attend_piece(): jnp.einsum('rqhe,rke->rqhk', query_rows, page_rows[:, :, 0], preferred_el...]
    all_to_all x1 -> x0, starting transfers between devices: 4.24 us -> none  [per_device(): lax.all_to_all(result.reshape(arrived_rows.shape), ('ctx', 'exp'), split_...]
    reduce_sum x5 -> x0, other arithmetic: 3.21 us -> none  [the longest x1 1.29 us: attend_piece(): totals = jnp.sum(weights, axis=-1)]
  transfers between devices with their start and end apart: 3 -> 0, of which waited for: 3 -> 0; matrix products, arithmetic and copies ran while one was open for 3% -> 0% of each run, Pallas kernels for 0% -> 0%
where the time goes in v1:
time: 74 us; the launch traced here: 73.7 us
  Pallas kernels  67.3 us (91%)
  local copies, waits for them, and re-layouts  5.75 us (8%)
    pallas_call x1, Pallas kernels, fused_device(): pl.pallas_call(functools.partial(fused_kernel, ctx_count, exp_count, capa...  67.3 us
    unnamed x2, local copies, waits for them, and re-layouts  3.04 us

profile of v1, /device:TPU:0, one launch (start us, length us, event | category | flops | bytes accessed | tf_op | source)
XLA Modules:
  0.0 73.7 jit_solution(8144767496579501389)
XLA Ops:
  0.6 1.4 %copy.12.ids = s32[16,8]{1,0:T(8,128)} copy(s32[16,8]{0,1:T(8,128)} %bitcast.19) | data formatting | bytes 1024 | tf_op jit(solution)/shard_map/squeeze | solution.py:556
  2.0 1.4 %copy.13.scores = f32[16,8]{1,0:T(8,128)} copy(f32[16,8]{0,1:T(8,128)} %bitcast.20) | data formatting | bytes 1024 | tf_op jit(solution)/shard_map/squeeze | solution.py:556
  3.3 67.3 %shard_map.113 = (bf16[64,1024]{1,0:T(8,128)(2,1)}, bf16[16,2048]{1,0:T(8,128)(2,1)}) custom-call(s32[4]{0:T(128)} %bitcast.21, bf16[64,1024]{1,0:T(8,128)(2,1)} %bitcast.14, bf16[576,2,128]{2,1,0:T(2,128)(2,1)} %bitcast.13, bf16[16,2048]{1,0:T(8,128)(2,1)} %bitcast.16, f32[1,2048]{1,0:T(1,128)} %bitcast.18, s32[16,8]{1,0:T(8,128)} %copy.12.ids, ...), custom_call_target="tpu_custom_call" | custom-call | tf_op jit(solution)/shard_map/pallas_call | solution.py:505
  70.7 1.6 %copy.16 = bf16[1,64,1024]{2,1,0:T(8,128)(2,1)} copy(bf16[1,64,1024]{2,1,0:T(8,128)(2,1)} %bitcast.15) | data formatting | bytes 262144
  72.3 1.5 %copy.17 = bf16[1,16,2048]{2,1,0:T(8,128)(2,1)} copy(bf16[1,16,2048]{2,1,0:T(8,128)(2,1)} %bitcast.17) | data formatting | bytes 131072

commit v2 on v1

--- a/solution.py
+++ b/solution.py
@@ -191,7 +191,7 @@
     context_out, layer_out,
     kv, q_rows, bias, peak, total, accum, wo, wi, wg, wu, wd,
     ids_all, scores_all, combine_all, place, gather,
-    rs_full, rs_send, rs_recv, hidden, nz, x_send, x_recv, x_rows, y_send, y_recv, y_rows, mix_send, mix_recv,
+    rs_full, rs_send, rs_recv, hidden, nz, x_send, x_recv, x_rows, y_send, y_recv, mix_send, mix_recv,
     kv_left, kv_right, kv_recv, w_sem,
     ids_s, ids_r, sc_s, sc_r, rs_s, rs_r, nz_s, nz_r, dx_s, dx_r, ret_s, ret_r, mix_s, mix_r,
 ):
@@ -203,7 +203,9 @@
     slab = page_size - fresh
     rows = residual.shape[0]
     width = residual.shape[1]
-    top = ids.shape[1]
+    top = ids.shape[0]
+    chunks = kv.shape[1]
+    chunk = kv.shape[2]
     scaling = HEAD ** (-0.5) * 1.4426950408889634
 
     def ctx_peer(k):
@@ -230,19 +232,30 @@
         pl.semaphore_signal(barrier, inc=1, device_id=exp_peer(k), device_id_type=MESH)
     pl.semaphore_wait(barrier, ctx_count + exp_count - 2)
 
-    def right_copy(src, p):
-        return remote(src, kv.at[p], kv_right.at[p], kv_recv.at[p], {"ctx": ci + 1})
-
-    def left_copy(src, p):
-        return remote(src, kv.at[p], kv_left.at[p], kv_recv.at[p], {"ctx": ci - 1})
-
-    @pl.when(ci < ctx_count - 1)
-    def _():
-        right_copy(page, ci).start()
-
-    @pl.when(ci > 0)
-    def _():
-        left_copy(page, ci).start()
+    def piece_of(p, c, first):
+        return page.at[pl.ds(c * chunk, chunk)] if first else kv.at[p, c]
+
+    def right_copy(p, c, first=False):
+        return remote(piece_of(p, c, first), kv.at[p, c], kv_right.at[p, c], kv_recv.at[p, c], {"ctx": ci + 1})
+
+    def left_copy(p, c, first=False):
+        return remote(piece_of(p, c, first), kv.at[p, c], kv_left.at[p, c], kv_recv.at[p, c], {"ctx": ci - 1})
+
+    for c in range(chunks):
+        @pl.when(ci < ctx_count - 1)
+        def _():
+            right_copy(ci, c, True).start()
+
+        @pl.when(ci > 0)
+        def _():
+            left_copy(ci, c, True).start()
+
+    own_page = [
+        pltpu.make_async_copy(page.at[pl.ds(c * chunk, chunk)], kv.at[ci, c], kv_recv.at[ci, c])
+        for c in range(chunks)
+    ]
+    for c in own_page:
+        c.start()
 
     small = []
     for k in range(1, ctx_count):
@@ -259,14 +272,16 @@
     total[...] = jnp.zeros_like(total)
     peak[...] = jnp.full_like(peak, floor_value)
 
-    offset = lax.broadcasted_iota(jnp.int32, (fresh, page_size), 1)
-    position = lax.broadcasted_iota(jnp.int32, (fresh, page_size), 0) + ci * fresh
-
-    def attend(source, p):
-        live = lengths[p]
-        cached = (offset < slab) & (offset < live)
+    step_rows = lax.broadcasted_iota(jnp.int32, (fresh, chunk), 1)
+    position = lax.broadcasted_iota(jnp.int32, (fresh, chunk), 0) + ci * fresh
+
+    def mask(p, c):
+        offset = step_rows + c * chunk
+        cached = (offset < slab) & (offset < lengths[p])
         new = (offset >= slab) & (p * fresh + offset - slab <= position)
         bias[...] = jnp.where(cached | new, 0.0, floor_value)
+
+    def attend(source):
         both = source[...]
         keys = both[:, 0, :]
         values = both[:, 1, :]
@@ -287,7 +302,15 @@
             )
             peak[sl, :] = now
 
-    attend(page, ci)
+    for c in range(chunks):
+        own_page[c].wait()
+
+    def own_chunk(c, carry):
+        mask(ci, c)
+        attend(kv.at[ci, c])
+        return carry
+
+    lax.fori_loop(0, chunks, own_chunk, 0)
 
     copies_w[1].wait()
     depth = 256
@@ -301,56 +324,58 @@
 
     lax.fori_loop(0, width // depth, unpack, 0)
 
-    combined = scores[...] / jnp.sum(scores[...], axis=1, keepdims=True)
+    combined = scores[...] / jnp.sum(scores[...], axis=0, keepdims=True)
     ids_all[0] = ids[...]
     combine_all[0] = combined.astype(BF).astype(F32)
     for c in small:
         c.wait()
     for k in range(1, ctx_count):
         given = scores_all[k]
-        combine_all[k] = (given / jnp.sum(given, axis=1, keepdims=True)).astype(BF).astype(F32)
+        combine_all[k] = (given / jnp.sum(given, axis=0, keepdims=True)).astype(BF).astype(F32)
 
     lanes = exp_count * capacity
-    lane = lax.broadcasted_iota(jnp.int32, (rows, lanes), 1)
+    lane = lax.broadcasted_iota(jnp.int32, (lanes, rows), 0)
     wanted = ci * exp_count + lax.rem(ei + lane // capacity, exp_count)
     seat = (lane - lane // capacity * capacity).astype(F32)
     earlier = (
-        lax.broadcasted_iota(jnp.int32, (rows, rows), 1)
-        < lax.broadcasted_iota(jnp.int32, (rows, rows), 0)
+        lax.broadcasted_iota(jnp.int32, (rows, rows), 0)
+        < lax.broadcasted_iota(jnp.int32, (rows, rows), 1)
     ).astype(F32)
     for k in range(ctx_count):
-        chosen = jnp.zeros((rows, lanes), F32)
-        portion = jnp.zeros((rows, lanes), F32)
+        chosen = jnp.zeros((lanes, rows), F32)
+        portion = jnp.zeros((lanes, rows), F32)
         for j in range(top):
-            hit = ids_all[k, :, j:j + 1] == wanted
+            hit = ids_all[k, j:j + 1, :] == wanted
             chosen = jnp.where(hit, 1.0, chosen)
-            portion = jnp.where(hit, combine_all[k, :, j:j + 1], portion)
-        rank = jnp.dot(earlier.astype(BF), chosen.astype(BF), preferred_element_type=F32)
+            portion = jnp.where(hit, combine_all[k, j:j + 1, :], portion)
+        rank = jnp.dot(chosen.astype(BF), earlier.astype(BF), preferred_element_type=F32)
         seated = (chosen > 0.5) & (rank == seat)
         place[k] = jnp.where(seated, 1.0, 0.0)
         gather[k] = jnp.where(seated, portion, 0.0)
 
     def arrival(i, carry):
-        d = i // 2 + 1
+        d = i // (2 * chunks) + 1
+        c = lax.rem(i // 2, chunks)
         p = jnp.where(lax.rem(i, 2) == 0, ci - d, ci + d)
 
         @pl.when((p >= 0) & (p < ctx_count))
         def _():
-            right_copy(kv.at[p], p).wait_recv()
+            mask(p, c)
+            right_copy(p, c).wait_recv()
 
             @pl.when((p < ci) & (ci < ctx_count - 1))
             def _():
-                right_copy(kv.at[p], p).start()
+                right_copy(p, c).start()
 
             @pl.when((p > ci) & (ci > 0))
             def _():
-                left_copy(kv.at[p], p).start()
-
-            attend(kv.at[p], p)
+                left_copy(p, c).start()
+
+            attend(kv.at[p, c])
 
         return carry
 
-    lax.fori_loop(0, 2 * (ctx_count - 1), arrival, 0)
+    lax.fori_loop(0, 2 * (ctx_count - 1) * chunks, arrival, 0)
 
     for h in range(heads):
         sl = slice(h * fresh, (h + 1) * fresh)
@@ -395,12 +420,17 @@
         nz_copies[k] = c
 
     dx_copies = []
-    for k in [0] + order:
+    ret_copies = []
+    mix_copies = {}
+    own = None
+    places = [0] + order
+    half = (ctx_count + 1) // 2
+    stages = [g for g in (places[:half], places[half:]) if g]
+
+    def dispatch(k):
         if k:
             nz_copies[k].wait_recv()
-        routed = lax.dot_general(
-            place[k].astype(BF), nz[k], (((0,), (0,)), ((), ())), preferred_element_type=F32
-        )
+        routed = jnp.dot(place[k].astype(BF), nz[k], preferred_element_type=F32)
         for j in range(exp_count):
             block = routed[j * capacity:(j + 1) * capacity].astype(BF)
             if j == 0:
@@ -410,76 +440,96 @@
                 c = remote(x_send.at[j, k], x_recv.at[j, k], dx_s.at[j, k], dx_r.at[j, k], exp_peer(j))
                 c.start()
                 dx_copies.append(c)
+
+    def experts(group):
+        for k in group:
+            for j in range(1, exp_count):
+                dx_copies[places.index(k) * (exp_count - 1) + j - 1].wait_recv()
+        count = len(group) * exp_count * capacity
+        for j in range(exp_count):
+            for n, k in enumerate(group):
+                at = slice((j * len(group) + n) * capacity, (j * len(group) + n + 1) * capacity)
+                x_rows[at, :] = x_recv[j, k].astype(F32)
+        x = x_rows[:count, :].astype(BF)
+        gate = jnp.dot(x, wg[...], preferred_element_type=F32)
+        up = jnp.dot(x, wu[...], preferred_element_type=F32)
+        act = (gate / (1.0 + jnp.exp(-gate)) * up).astype(BF)
+        result = jnp.dot(act, wd[...], preferred_element_type=F32)
+        for n, k in enumerate(group):
+            for j in range(exp_count):
+                first = (j * len(group) + n) * capacity
+                block = result[first:first + capacity].astype(BF)
+                if j == 0:
+                    y_recv[0, k] = block
+                else:
+                    y_send[j, k] = block
+                    c = remote(y_send.at[j, k], y_recv.at[j, k], ret_s.at[j, k], ret_r.at[j, k], exp_peer(exp_count - j))
+                    c.start()
+                    ret_copies.append(c)
+
+    def mixing(k):
+        for j in range(1, exp_count):
+            ret_copies[places.index(k) * (exp_count - 1) + j - 1].wait_recv()
+        rows_k = jnp.concatenate([y_recv[j, k].astype(F32) for j in range(exp_count)], 0).astype(BF)
+        mixed = lax.dot_general(
+            gather[k].astype(BF), rows_k, (((0,), (0,)), ((), ())), preferred_element_type=F32
+        )
+        if k == 0:
+            return mixed
+        mix_send[k] = mixed.astype(BF)
+        c = remote(mix_send.at[k], mix_recv.at[k], mix_s.at[k], mix_r.at[k], ctx_peer(ctx_count - k))
+        c.start()
+        mix_copies[k] = c
+
+    for k in stages[0]:
+        dispatch(k)
     copies_w[2].wait()
-    for c in dx_copies:
-        c.wait_recv()
-    for j in range(exp_count):
-        for k in range(ctx_count):
-            at = slice((j * ctx_count + k) * capacity, (j * ctx_count + k + 1) * capacity)
-            x_rows[at, :] = x_recv[j, k].astype(F32)
-    x = x_rows[...].astype(BF)
-    gate = jnp.dot(x, wg[...], preferred_element_type=F32)
-    up = jnp.dot(x, wu[...], preferred_element_type=F32)
-    act = (gate / (1.0 + jnp.exp(-gate)) * up).astype(BF)
-    span = ctx_count * capacity
-    ret_copies = []
-    result = jnp.dot(act, wd[...], preferred_element_type=F32)
-    for j in range(exp_count):
-        block = result[j * span:(j + 1) * span].astype(BF)
-        if j == 0:
-            y_recv[0] = block
-        else:
-            y_send[j] = block
-            c = remote(y_send.at[j], y_recv.at[j], ret_s.at[j], ret_r.at[j], exp_peer(exp_count - j))
-            c.start()
-            ret_copies.append(c)
-    for c in ret_copies:
-        c.wait_recv()
-    for j in range(exp_count):
-        y_rows[j] = y_recv[j].astype(F32)
-    mix_copies = []
-    own = None
-    for k in list(reversed(order)) + [0]:
-        rows_k = jnp.concatenate(
-            [y_rows[j, k * capacity:(k + 1) * capacity] for j in range(exp_count)], 0
-        ).astype(BF)
-        mixed = jnp.dot(gather[k].astype(BF), rows_k, preferred_element_type=F32)
-        if k == 0:
-            own = mixed
-        else:
-            mix_send[k] = mixed.astype(BF)
-            c = remote(mix_send.at[k], mix_recv.at[k], mix_s.at[k], mix_r.at[k], ctx_peer(ctx_count - k))
-            c.start()
-            mix_copies.append(c)
+    experts(stages[0])
+    for group in stages[1:]:
+        for k in group:
+            dispatch(k)
+        experts(group)
+    for k in places[1:]:
+        mixing(k)
+    own = mixing(0)
     out = hidden[...].astype(F32) + own
-    for c, k in zip(reversed(mix_copies), order):
-        c.wait_recv()
+    for k in order:
+        mix_copies[k].wait_recv()
         out = out + mix_recv[k].astype(F32)
     layer_out[...] = out.astype(BF)
 
-    for c in rs_copies + list(nz_copies.values()) + dx_copies + ret_copies + mix_copies:
+    for c in rs_copies + list(nz_copies.values()) + dx_copies + ret_copies + list(mix_copies.values()):
         c.wait_send()
 
-    @pl.when(ci < ctx_count - 1)
-    def _():
-        right_copy(page, ci).wait_send()
-
-    @pl.when(ci > 0)
-    def _():
-        left_copy(page, ci).wait_send()
-
-    def drain(p, carry):
+    for c in range(chunks):
+        @pl.when(ci < ctx_count - 1)
+        def _():
+            right_copy(ci, c, True).wait_send()
+
+        @pl.when(ci > 0)
+        def _():
+            left_copy(ci, c, True).wait_send()
+
+    def drain(i, carry):
+        p = i // chunks
+        c = lax.rem(i, chunks)
+
         @pl.when((p < ci) & (ci < ctx_count - 1))
         def _():
-            right_copy(kv.at[p], p).wait_send()
+            right_copy(p, c).wait_send()
 
         @pl.when((p > ci) & (ci > 0))
         def _():
-            left_copy(kv.at[p], p).wait_send()
+            left_copy(p, c).wait_send()
 
         return carry
 
-    lax.fori_loop(0, ctx_count, drain, 0)
+    lax.fori_loop(0, ctx_count * chunks, drain, 0)
+
+
+def settle(context, layer, context_out, layer_out):
+    context_out[...] = context[...]
+    layer_out[...] = layer[...]
 
 
 def fused_device(
@@ -502,18 +552,19 @@
     V = pltpu.VMEM
     lanes = exp_count * capacity
     pieces = 4
+    chunks = next(n for n in (3, 2, 1) if page_size % (16 * n) == 0 or n == 1)
     context, layer_out = pl.pallas_call(
         functools.partial(fused_kernel, ctx_count, exp_count, capacity),
         out_shape=(
             jax.ShapeDtypeStruct((fresh, query_width), BF),
             jax.ShapeDtypeStruct((rows, width), BF),
         ),
-        in_specs=[sm, vm, vm, vm, vm, vm, vm, hbm, hbm, hbm],
+        in_specs=[sm, vm, hbm, vm, vm, vm, vm, hbm, hbm, hbm],
         out_specs=(vm, vm),
         scratch_shapes=[
-            V((ctx_count,) + pages.shape[1:], BF),
+            V((ctx_count, chunks, page_size // chunks) + pages.shape[2:], BF),
             V((stacked, HEAD), BF),
-            V((fresh, page_size), F32),
+            V((fresh, page_size // chunks), F32),
             V((stacked, HEAD), F32),
             V((stacked, HEAD), F32),
             V((stacked, HEAD), F32),
@@ -522,11 +573,11 @@
             V((width, hidden_width), BF),
             V((width, hidden_width), BF),
             V(expert_output.shape[1:], BF),
-            V((ctx_count, rows, top), jnp.int32),
-            V((ctx_count, rows, top), F32),
-            V((ctx_count, rows, top), F32),
-            V((ctx_count, rows, lanes), F32),
-            V((ctx_count, rows, lanes), F32),
+            V((ctx_count, top, rows), jnp.int32),
+            V((ctx_count, top, rows), F32),
+            V((ctx_count, top, rows), F32),
+            V((ctx_count, lanes, rows), F32),
+            V((ctx_count, lanes, rows), F32),
             V((pieces, fresh, width // pieces), F32),
             V((exp_count, pieces, rows, width // pieces), BF),
             V((exp_count, pieces, rows, width // pieces), BF),
@@ -535,17 +586,16 @@
             V((exp_count, ctx_count, capacity, width), BF),
             V((exp_count, ctx_count, capacity, width), BF),
             V((exp_count * span, width), F32),
-            V((exp_count, span, width), BF),
-            V((exp_count, span, width), BF),
-            V((exp_count, span, width), F32),
+            V((exp_count, ctx_count, capacity, width), BF),
+            V((exp_count, ctx_count, capacity, width), BF),
             V((ctx_count, rows, width), BF),
             V((ctx_count, rows, width), BF),
-            dma((ctx_count,)), dma((ctx_count,)), dma((ctx_count,)), dma((3,)),
+            dma((ctx_count, chunks)), dma((ctx_count, chunks)), dma((ctx_count, chunks)), dma((3,)),
             dma((ctx_count,)), dma((ctx_count,)), dma((ctx_count,)), dma((ctx_count,)),
             dma((exp_count, pieces)), dma((exp_count, pieces)),
             dma((ctx_count,)), dma((ctx_count,)),
             dma((exp_count, ctx_count)), dma((exp_count, ctx_count)),
-            dma((exp_count,)), dma((exp_count,)),
+            dma((exp_count, ctx_count)), dma((exp_count, ctx_count)),
             dma((ctx_count,)), dma((ctx_count,)),
         ],
         compiler_params=pltpu.CompilerParams(
@@ -553,8 +603,17 @@
         ),
     )(
         cached_lengths[0], queries[0], pages[0], residual_in[0], norm_gain.reshape(1, width),
-        expert_ids[0], route_scores[0], out_weight, expert_input[0], expert_output[0],
-    )
+        expert_ids[0].T, route_scores[0].T, out_weight, expert_input[0], expert_output[0],
+    )
+    context, layer_out = pl.pallas_call(
+        settle,
+        out_shape=(
+            jax.ShapeDtypeStruct(context.shape, BF),
+            jax.ShapeDtypeStruct(layer_out.shape, BF),
+        ),
+        in_specs=[vm, vm],
+        out_specs=(vm, vm),
+    )(context, layer_out)
     return context[None], layer_out[None]
 
 

time: 74 us -> 71.4 us (0.965)
  local copies, waits for them, and re-layouts: 5.75 us -> 0 us
  Pallas kernels: 67.3 us -> 70.6 us
    unnamed x2 -> x0, local copies, waits for them, and re-layouts: 3.04 us -> none
    squeeze x2 -> x0, local copies, waits for them, and re-layouts: 2.71 us -> none  [the longest x1 1.36 us: fused_device(): expert_ids[0]]
    pallas_call x1, Pallas kernels: 67.3 us -> 69.1 us  [fused_device(): pl.pallas_call(functools.partial(fused_kernel, ctx_count, exp_count, capa...]
    pallas_call x0 -> x1, Pallas kernels: none -> 1.59 us  [fused_device(): pl.pallas_call(settle, out_shape=(jax.ShapeDtypeStruct(context.shape, BF)...]
where the time goes in v2:
time: 71.4 us; the launch traced here: 71.3 us
  Pallas kernels  70.6 us (99%)
    pallas_call x1, Pallas kernels, fused_device(): pl.pallas_call(functools.partial(fused_kernel, ctx_count, exp_count, capa...  69.1 us
    pallas_call x1, Pallas kernels, fused_device(): pl.pallas_call(settle, out_shape=(jax.ShapeDtypeStruct(context.shape, BF)...  1.59 us

profile of v2, /device:TPU:0, one launch (start us, length us, event | category | flops | bytes accessed | tf_op | source)
XLA Modules:
  0.0 71.3 jit_solution(9927795001652669513)
XLA Ops:
  0.6 69.1 %shard_map.113 = (bf16[64,1024]{1,0:T(8,128)(2,1)}, bf16[16,2048]{1,0:T(8,128)(2,1)}) custom-call(s32[4]{0:T(128)} %bitcast.23, bf16[64,1024]{1,0:T(8,128)(2,1)} %bitcast.18, bf16[576,2,128]{2,1,0:T(2,128)(2,1)} %bitcast.17, bf16[16,2048]{1,0:T(8,128)(2,1)} %bitcast.19, f32[1,2048]{1,0:T(1,128)} %bitcast.20, s32[8,16]{1,0:T(8,128)} %bitcast.21, ...), custom_call_target="tpu_custom_call" | custom-call | tf_op jit(solution)/shard_map/pallas_call | solution.py:556
  69.7 1.6 %shard_map.114 = (bf16[64,1024]{1,0:T(8,128)(2,1)}, bf16[16,2048]{1,0:T(8,128)(2,1)}) custom-call(bf16[64,1024]{1,0:T(8,128)(2,1)} %get-tuple-element.6.context, bf16[16,2048]{1,0:T(8,128)(2,1)} %get-tuple-element.7.layer), custom_call_target="tpu_custom_call" | custom-call | tf_op jit(solution)/shard_map/pallas_call | solution.py:608

commit v3 on v2

--- a/solution.py
+++ b/solution.py
@@ -189,7 +189,7 @@
     ctx_count, exp_count, capacity,
     lengths, query, page, residual, gain, ids, scores, w_out, w_in, w_down,
     context_out, layer_out,
-    kv, q_rows, bias, peak, total, accum, wo, wi, wg, wu, wd,
+    kv, raw, q_rows, bias, peak, total, accum, wo, wi, wg, wu, wd,
     ids_all, scores_all, combine_all, place, gather,
     rs_full, rs_send, rs_recv, hidden, nz, x_send, x_recv, x_rows, y_send, y_recv, mix_send, mix_recv,
     kv_left, kv_right, kv_recv, w_sem,
@@ -225,37 +225,39 @@
         pltpu.make_async_copy(w_down, wd, w_sem.at[2]),
     ]
 
+    own_page = [
+        pltpu.make_async_copy(page.at[pl.ds(c * chunk, chunk)], raw.at[c], kv_recv.at[ci, c])
+        for c in range(chunks)
+    ]
+    for c in own_page:
+        c.start()
+
     barrier = pltpu.get_barrier_semaphore()
     for k in range(1, ctx_count):
         pl.semaphore_signal(barrier, inc=1, device_id=ctx_peer(k), device_id_type=MESH)
     for k in range(1, exp_count):
         pl.semaphore_signal(barrier, inc=1, device_id=exp_peer(k), device_id_type=MESH)
+    for c in range(chunks):
+        own_page[c].wait()
+        both = raw[c]
+        kv[ci, c, :, :HEAD] = both[:, 0, :]
+        kv[ci, c, :, HEAD:] = both[:, 1, :]
     pl.semaphore_wait(barrier, ctx_count + exp_count - 2)
 
-    def piece_of(p, c, first):
-        return page.at[pl.ds(c * chunk, chunk)] if first else kv.at[p, c]
-
-    def right_copy(p, c, first=False):
-        return remote(piece_of(p, c, first), kv.at[p, c], kv_right.at[p, c], kv_recv.at[p, c], {"ctx": ci + 1})
-
-    def left_copy(p, c, first=False):
-        return remote(piece_of(p, c, first), kv.at[p, c], kv_left.at[p, c], kv_recv.at[p, c], {"ctx": ci - 1})
+    def right_copy(p, c):
+        return remote(kv.at[p, c], kv.at[p, c], kv_right.at[p, c], kv_recv.at[p, c], {"ctx": ci + 1})
+
+    def left_copy(p, c):
+        return remote(kv.at[p, c], kv.at[p, c], kv_left.at[p, c], kv_recv.at[p, c], {"ctx": ci - 1})
 
     for c in range(chunks):
         @pl.when(ci < ctx_count - 1)
         def _():
-            right_copy(ci, c, True).start()
+            right_copy(ci, c).start()
 
         @pl.when(ci > 0)
         def _():
-            left_copy(ci, c, True).start()
-
-    own_page = [
-        pltpu.make_async_copy(page.at[pl.ds(c * chunk, chunk)], kv.at[ci, c], kv_recv.at[ci, c])
-        for c in range(chunks)
-    ]
-    for c in own_page:
-        c.start()
+            left_copy(ci, c).start()
 
     small = []
     for k in range(1, ctx_count):
@@ -282,9 +284,8 @@
         bias[...] = jnp.where(cached | new, 0.0, floor_value)
 
     def attend(source):
-        both = source[...]
-        keys = both[:, 0, :]
-        values = both[:, 1, :]
+        keys = source[:, :HEAD]
+        values = source[:, HEAD:]
         step = 2 if heads % 2 == 0 else 1
         for h in range(0, heads, step):
             sl = slice(h * fresh, (h + step) * fresh)
@@ -301,9 +302,6 @@
                 w.astype(BF), values, preferred_element_type=F32
             )
             peak[sl, :] = now
-
-    for c in range(chunks):
-        own_page[c].wait()
 
     def own_chunk(c, carry):
         mask(ci, c)
@@ -424,8 +422,7 @@
     mix_copies = {}
     own = None
     places = [0] + order
-    half = (ctx_count + 1) // 2
-    stages = [g for g in (places[:half], places[half:]) if g]
+    stages = [places]
 
     def dispatch(k):
         if k:
@@ -504,11 +501,11 @@
     for c in range(chunks):
         @pl.when(ci < ctx_count - 1)
         def _():
-            right_copy(ci, c, True).wait_send()
+            right_copy(ci, c).wait_send()
 
         @pl.when(ci > 0)
         def _():
-            left_copy(ci, c, True).wait_send()
+            left_copy(ci, c).wait_send()
 
     def drain(i, carry):
         p = i // chunks
@@ -562,7 +559,8 @@
         in_specs=[sm, vm, hbm, vm, vm, vm, vm, hbm, hbm, hbm],
         out_specs=(vm, vm),
         scratch_shapes=[
-            V((ctx_count, chunks, page_size // chunks) + pages.shape[2:], BF),
+            V((ctx_count, chunks, page_size // chunks, 2 * HEAD), BF),
+            V((chunks, page_size // chunks) + pages.shape[2:], BF),
             V((stacked, HEAD), BF),
             V((fresh, page_size // chunks), F32),
             V((stacked, HEAD), F32),

time: 71.4 us -> 67.5 us (0.945)
  Pallas kernels: 70.6 us -> 66.7 us
    pallas_call x1, Pallas kernels: 69.1 us -> 65.1 us  [fused_device(): pl.pallas_call(functools.partial(fused_kernel, ctx_count, exp_count, capa...]
where the time goes in v3:
time: 67.5 us; the launch traced here: 67.3 us
  Pallas kernels  66.7 us (99%)
    pallas_call x1, Pallas kernels, fused_device(): pl.pallas_call(functools.partial(fused_kernel, ctx_count, exp_count, capa...  65.1 us
    pallas_call x1, Pallas kernels, fused_device(): pl.pallas_call(settle, out_shape=(jax.ShapeDtypeStruct(context.shape, BF)...  1.59 us

profile of v3, /device:TPU:0, one launch (start us, length us, event | category | flops | bytes accessed | tf_op | source)
XLA Modules:
  0.0 67.3 jit_solution(8062299655796407850)
XLA Ops:
  0.6 65.1 %shard_map.113 = (bf16[64,1024]{1,0:T(8,128)(2,1)}, bf16[16,2048]{1,0:T(8,128)(2,1)}) custom-call(s32[4]{0:T(128)} %bitcast.23, bf16[64,1024]{1,0:T(8,128)(2,1)} %bitcast.18, bf16[576,2,128]{2,1,0:T(2,128)(2,1)} %bitcast.17, bf16[16,2048]{1,0:T(8,128)(2,1)} %bitcast.19, f32[1,2048]{1,0:T(1,128)} %bitcast.20, s32[8,16]{1,0:T(8,128)} %bitcast.21, ...), custom_call_target="tpu_custom_call" | custom-call | tf_op jit(solution)/shard_map/pallas_call | solution.py:553
  65.7 1.6 %shard_map.114 = (bf16[64,1024]{1,0:T(8,128)(2,1)}, bf16[16,2048]{1,0:T(8,128)(2,1)}) custom-call(bf16[64,1024]{1,0:T(8,128)(2,1)} %get-tuple-element.6.context, bf16[16,2048]{1,0:T(8,128)(2,1)} %get-tuple-element.7.layer), custom_call_target="tpu_custom_call" | custom-call | tf_op jit(solution)/shard_map/pallas_call | solution.py:606
